TPU v7x, 32 devices: a whole 2x2x4 slice. The times are simulated.
32 devices in a mesh: dp: 4 (over y, core), row: 2 (over x), col: 4 (over z).
Axes of the slice: x: 2, y: 2, z: 4, core: 2. Of those that a mesh axis runs over, the one named last changes fastest.
Arguments:
- tokens: bfloat16 [12288, 768], P(('dp', 'col'), 'row'), may hold values from -6 to 6
- cotangent: bfloat16 [12288, 768], P(('dp', 'col'), 'row'), may hold values from -6 to 6
- timestep: int32 [4], P('dp'), may hold values from 0 to 999
- piece_starts: int32 [4, 4], P('dp'), may hold values from 0 to 2816, as said below
- w_mod: bfloat16 [128, 6, 768], P(None, None, 'row'), may hold values from -0.5 to 0.5
- b_mod: float32 [6, 768], P(None, 'row'), may hold values from -3 to 3
- gain_attn: float32 [768], P('row'), may hold values from 0.5 to 1.5
- w_qkv: bfloat16 [2304, 768], P('col', 'row'), may hold values from -0.21875 to 0.21875
- w_out: bfloat16 [768, 768], P('col', 'row'), may hold values from -0.875 to 0.875
- gain_mlp: float32 [768], P('row'), may hold values from 0.5 to 1.5
- w_up: bfloat16 [768, 3072], P('row', 'col'), may hold values from -0.21875 to 0.21875
- b_up: bfloat16 [3072], P('col'), may hold values from -3 to 3
- w_down: bfloat16 [3072, 768], P('col', 'row'), may hold values from -0.109375 to 0.109375
- b_down: float32 [768], P('row'), may hold values from -3 to 3
Outputs:
- block_out: bfloat16 [12288, 768], P(('dp', 'col'), 'row')
- d_tokens: float32 [12288, 768], P(('dp', 'col'), 'row')
- d_mod_w: float32 [128, 6, 768], P(None, None, 'row')
- d_mod_b: float32 [6, 768], P(None, 'row')
- d_gain_attn: float32 [768], P('row')
- d_qkv: float32 [2304, 768], P('col', 'row')
- d_out_proj: float32 [768, 768], P('col', 'row')
- d_gain_mlp: float32 [768], P('row')
- d_up: float32 [768, 3072], P('row', 'col')
- d_up_bias: float32 [3072], P('col')
- d_down: float32 [3072, 768], P('col', 'row')
- d_down_bias: float32 [768], P('row')
Inputs may be any that keep to these rules, and one draw needn't show every extreme that they name: `piece_starts`: in every sequence the 4 pieces of 256 tokens rise, do not intersect and lie inside the sequence; the first opens the sequence and the last closes it.
All inputs are finite; a program needn't handle non-finite values.
Results may differ from a plain program's by a relative error of at most 0.014.
The roundings to bfloat16 on the way count: a program that leaves them out, or rounds other values in their place, can miss the bound.
Values may be sent and summed in bfloat16 or wider, within the bound.
No kernel may reach another device: no remote copies, remote signals or barrier semaphores. Data moves between devices by JAX's collectives and lax.ppermute only.
A program may use at most 192 MiB of HBM per device.

v0:
```python
import math
import jax
import jax.numpy as jnp
from jax import lax
from jax.sharding import PartitionSpec as P

D = 768
HEAD = 64
COND = 128
PIECE = 256
PIECES = 4
precise = lax.Precision.HIGHEST
epsilon = 1e-05


def embed_time(time_step):
    half_size = COND // 2
    frequency = jnp.exp(-math.log(10000.0) * jnp.arange(half_size, dtype=jnp.float32) / half_size)
    angles = time_step * frequency
    return jax.nn.silu(jnp.concatenate([jnp.cos(angles), jnp.sin(angles)]))


def rotate(vectors, places):
    half_size = HEAD // 2
    frequency = jnp.exp(-math.log(10000.0) * jnp.arange(half_size, dtype=jnp.float32) / half_size)
    angles = places.astype(jnp.float32)[:, None] * frequency[None, :]
    cosine = jnp.cos(angles)[:, None, :]
    sine_part = jnp.sin(angles)[:, None, :]
    first_half = vectors[..., :half_size]
    second_half = vectors[..., half_size:]
    return jnp.concatenate(
        [
            first_half * cosine - second_half * sine_part,
            second_half * cosine + first_half * sine_part,
        ],
        -1,
    )


def piece_ids(places, starts):
    inside = (places[:, None] >= starts[None, :]) & (places[:, None] < starts[None, :] + PIECE)
    labels = jnp.arange(1, PIECES + 1, dtype=jnp.int32)[None, :]
    return jnp.sum(jnp.where(inside, labels, 0), axis=1) - 1


def visible(query_places, seq_len, starts):
    key_places = jnp.arange(seq_len, dtype=jnp.int32)
    query_piece = piece_ids(query_places, starts)
    key_piece = piece_ids(key_places, starts)
    return (key_places[None, :] <= query_places[:, None]) | (
        query_piece[:, None] == key_piece[None, :]
    ) & (query_piece[:, None] >= 0)


def into_heads(activation, weight, contract):
    gathered = lax.all_gather(activation, "col", axis=0, tiled=True)
    share_rows = gathered.shape[0] // lax.axis_size("row")

    def partial_product(start_row, row_count):
        return lax.dot_general(
            gathered, weight, (((1,), (contract,)), ((), ())), preferred_element_type=jnp.float32
        )

    return (
        lax.psum_scatter(
            partial_product(jnp.int32(0), share_rows * lax.axis_size("row")),
            "row",
            scatter_dimension=0,
            tiled=True,
        ),
        gathered,
    )


def into_stream(activation, weight, contract):
    gathered = lax.all_gather(activation, "row", axis=0, tiled=True)
    share_rows = gathered.shape[0] // lax.axis_size("col")

    def partial_product(start_row, row_count):
        return lax.dot_general(
            gathered, weight, (((1,), (contract,)), ((), ())), preferred_element_type=jnp.float32
        )

    return (
        lax.psum_scatter(
            partial_product(jnp.int32(0), share_rows * lax.axis_size("col")),
            "col",
            scatter_dimension=0,
            tiled=True,
        ),
        gathered,
    )


def weight_grad(first_operand, second_operand):
    return lax.dot_general(
        first_operand, second_operand, (((0,), (0,)), ((), ())), preferred_element_type=jnp.float32
    )


def row_totals(first_sum, second_sum):
    return lax.psum((first_sum, second_sum), "row")


def norm_forward(values, gain_vec, shift_vec, scale_vec, totals):
    row_total, row_square = totals(jnp.sum(values, -1), jnp.sum(values * values, -1))
    row_mean = row_total / D
    inv_std = lax.rsqrt(row_square / D - row_mean * row_mean + epsilon)
    normed = (values - row_mean[:, None]) * inv_std[:, None]
    return (
        normed,
        inv_std,
        (normed * gain_vec * (1.0 + scale_vec) + shift_vec).astype(jnp.bfloat16),
    )


def norm_backward(upstream, normed, inv_std, gain_vec, scale_vec, totals):
    d_shift = jnp.sum(upstream, 0)
    d_scale = jnp.sum(upstream * normed * gain_vec, 0)
    d_gain = jnp.sum(upstream * normed * (1.0 + scale_vec), 0)
    d_normed = upstream * gain_vec * (1.0 + scale_vec)
    mean_grad, mean_proj = totals(jnp.sum(d_normed, -1), jnp.sum(d_normed * normed, -1))
    d_values = inv_std[:, None] * (
        d_normed - mean_grad[:, None] / D - normed * mean_proj[:, None] / D
    )
    return (d_values, d_gain, d_shift, d_scale)


def attend(query_head, key_head, value_head, allowed):
    scores = lax.dot_general(
        query_head, key_head, (((1,), (1,)), ((), ())), preferred_element_type=jnp.float32
    ) * HEAD ** (-0.5)
    scores = jnp.where(allowed, scores, -1e30)
    row_max = jnp.max(scores, -1, keepdims=True)
    weights_raw = jnp.exp(scores - row_max)
    row_sum = jnp.sum(weights_raw, -1, keepdims=True)
    probabilities = (weights_raw / row_sum).astype(jnp.bfloat16)
    mixed_head = jnp.dot(probabilities, value_head, preferred_element_type=jnp.float32)
    return (mixed_head, (row_max + jnp.log(row_sum))[:, 0])


def attend_back(query_head, key_head, value_head, d_mixed_head, log_sum, allowed):
    scores = lax.dot_general(
        query_head, key_head, (((1,), (1,)), ((), ())), preferred_element_type=jnp.float32
    ) * HEAD ** (-0.5)
    probabilities = jnp.where(allowed, jnp.exp(scores - log_sum[:, None]), 0.0)
    d_prob = lax.dot_general(
        d_mixed_head, value_head, (((1,), (1,)), ((), ())), preferred_element_type=jnp.float32
    )
    d_scores = (
        probabilities * (d_prob - jnp.sum(probabilities * d_prob, -1, keepdims=True))
    ).astype(jnp.bfloat16)
    d_query = jnp.dot(d_scores, key_head, preferred_element_type=jnp.float32) * HEAD ** (-0.5)
    d_key = weight_grad(d_scores, query_head) * HEAD ** (-0.5)
    d_value = weight_grad(probabilities.astype(jnp.bfloat16), d_mixed_head)
    return (d_query, d_key, d_value)


def rotate_pair(projected, places):
    return jax.vjp(
        lambda first_in, second_in: (rotate(first_in, places), rotate(second_in, places)),
        projected[:, :, 0],
        projected[:, :, 1],
    )


def attention_forward(queries, key_value_all, allowed):
    heads_query = queries.transpose(1, 0, 2)
    heads_key = key_value_all[:, :, 0].transpose(1, 0, 2)
    heads_value = key_value_all[:, :, 1].transpose(1, 0, 2)
    mixed, log_sum = lax.map(
        lambda operands: attend(operands[0], operands[1], operands[2], allowed),
        (heads_query, heads_key, heads_value),
    )
    mixed = (
        mixed.transpose(1, 0, 2)
        .reshape(queries.shape[0], queries.shape[1] * HEAD)
        .astype(jnp.bfloat16)
    )
    return (mixed, log_sum, (heads_query, heads_key, heads_value))


def attention_backward(saved, d_mixed, log_sum, allowed):
    heads_query, heads_key, heads_value = saved
    head_count = heads_query.shape[0]
    query_rows = heads_query.shape[1]
    seq_len = heads_key.shape[1]
    d_mixed_heads = (
        d_mixed.astype(jnp.bfloat16).reshape(query_rows, head_count, HEAD).transpose(1, 0, 2)
    )
    d_query, d_key, d_value = lax.map(
        lambda operands: attend_back(
            operands[0], operands[1], operands[2], operands[3], operands[4], allowed
        ),
        (heads_query, heads_key, heads_value, d_mixed_heads, log_sum),
    )
    d_key_value = jnp.stack([d_key.transpose(1, 0, 2), d_value.transpose(1, 0, 2)], 2).reshape(
        seq_len, head_count * 2 * HEAD
    )
    return (d_query.transpose(1, 0, 2), d_key_value)


def small_stack(
    d_shift_attn,
    d_scale_attn,
    d_gate_attn,
    d_shift_mlp,
    d_scale_mlp,
    d_gate_mlp,
    d_gain_attn,
    d_gain_mlp,
    d_down_bias,
):
    return jnp.stack(
        [
            d_shift_attn,
            d_scale_attn,
            d_gate_attn,
            d_shift_mlp,
            d_scale_mlp,
            d_gate_mlp,
            d_gain_attn,
            d_gain_mlp,
            d_down_bias,
        ],
        0,
    )


def blocked_layer(
    tokens,
    cotangent,
    modulation,
    starts,
    gain_attn,
    w_qkv,
    w_out,
    gain_mlp,
    w_up,
    b_up,
    w_down,
    b_down,
):
    residual = tokens.astype(jnp.float32)
    shift_attn, scale_attn, gate_attn = (modulation[0], modulation[1], modulation[2])
    shift_mlp, scale_mlp, gate_mlp = (modulation[3], modulation[4], modulation[5])
    normed_one, inv_std_one, normed_in = norm_forward(
        residual, gain_attn, shift_attn, scale_attn, row_totals
    )
    projected, normed_in_all = into_heads(normed_in, w_qkv, 1)
    query_rows = projected.shape[0]
    heads_local = projected.shape[1] // (3 * HEAD)
    projected = projected.reshape(query_rows, heads_local, 3, HEAD)
    seq_len = query_rows * lax.axis_size("row")
    query_places = lax.axis_index("row") * query_rows + jnp.arange(query_rows, dtype=jnp.int32)
    rotated, rotate_back = rotate_pair(projected, query_places)
    queries = rotated[0].astype(jnp.bfloat16)
    key_value = jnp.stack(
        [rotated[1].astype(jnp.bfloat16), projected[:, :, 2].astype(jnp.bfloat16)], 2
    ).reshape(query_rows, heads_local * 2 * HEAD)
    key_value_all = lax.all_gather(key_value, "row", axis=0, tiled=True).reshape(
        seq_len, heads_local, 2, HEAD
    )
    allowed = visible(query_places, seq_len, starts)
    mixed, log_sum, saved = attention_forward(queries, key_value_all, allowed)
    attended, mixed_all = into_stream(mixed, w_out, 0)
    middle = residual + gate_attn * attended
    normed_two, inv_std_two, normed_mid = norm_forward(
        middle, gain_mlp, shift_mlp, scale_mlp, row_totals
    )
    hidden, normed_mid_all = into_heads(normed_mid, w_up, 0)
    hidden = hidden + b_up.astype(jnp.float32)
    active_full, gelu_back = jax.vjp(lambda inner: jax.nn.gelu(inner, approximate=True), hidden)
    active = active_full.astype(jnp.bfloat16)
    branch, active_all = into_stream(active, w_down, 0)
    branch = branch + b_down
    block_out = (middle + gate_mlp * branch).astype(jnp.bfloat16)
    upstream = cotangent.astype(jnp.float32)
    d_gate_mlp = jnp.sum(upstream * branch, 0)
    d_branch = (upstream * gate_mlp).astype(jnp.bfloat16)
    d_down_bias = jnp.sum(d_branch.astype(jnp.float32), 0)
    d_active, d_branch_all = into_heads(d_branch, w_down, 1)
    d_down = weight_grad(active_all, d_branch_all)
    d_hidden = gelu_back(d_active)[0].astype(jnp.bfloat16)
    d_up_bias = jnp.sum(d_hidden.astype(jnp.float32), 0)
    d_normed_mid, d_hidden_all = into_stream(d_hidden, w_up, 1)
    d_up = weight_grad(normed_mid_all, d_hidden_all)
    d_middle, d_gain_mlp, d_shift_mlp, d_scale_mlp = norm_backward(
        d_normed_mid, normed_two, inv_std_two, gain_mlp, scale_mlp, row_totals
    )
    d_middle = d_middle + upstream
    d_gate_attn = jnp.sum(d_middle * attended, 0)
    d_attended = (d_middle * gate_attn).astype(jnp.bfloat16)
    d_mixed, d_attended_all = into_heads(d_attended, w_out, 1)
    d_out_proj = weight_grad(mixed_all, d_attended_all)
    d_query, d_key_value = attention_backward(saved, d_mixed, log_sum, allowed)
    d_key_value = (
        lax.psum_scatter(d_key_value.astype(jnp.bfloat16), "row", scatter_dimension=0, tiled=True)
        .astype(jnp.float32)
        .reshape(query_rows, heads_local, 2, HEAD)
    )
    d_query_raw, d_key_raw = rotate_back((d_query, d_key_value[:, :, 0]))
    d_projected = (
        jnp.stack([d_query_raw, d_key_raw, d_key_value[:, :, 1]], 2)
        .reshape(query_rows, heads_local * 3 * HEAD)
        .astype(jnp.bfloat16)
    )
    d_normed_in, d_projected_all = into_stream(d_projected, w_qkv, 0)
    d_qkv = weight_grad(d_projected_all, normed_in_all)
    d_input, d_gain_attn, d_shift_attn, d_scale_attn = norm_backward(
        d_normed_in, normed_one, inv_std_one, gain_attn, scale_attn, row_totals
    )
    d_tokens = d_input + d_middle
    small_rows = small_stack(
        d_shift_attn,
        d_scale_attn,
        d_gate_attn,
        d_shift_mlp,
        d_scale_mlp,
        d_gate_mlp,
        d_gain_attn,
        d_gain_mlp,
        d_down_bias,
    )
    row_here = lax.axis_index("row")
    col_here = lax.axis_index("col")
    row_slots = jnp.where(
        (jnp.arange(lax.axis_size("row"), dtype=jnp.int32) == row_here)[:, None, None],
        small_rows[None],
        0.0,
    )
    col_slots = jnp.where(
        (jnp.arange(lax.axis_size("col"), dtype=jnp.int32) == col_here)[:, None],
        d_up_bias[None],
        0.0,
    )
    row_slots, col_slots = lax.psum((row_slots, col_slots), ("row", "col"))
    small_rows = lax.dynamic_index_in_dim(row_slots, row_here, 0, keepdims=False)
    d_up_bias = lax.dynamic_index_in_dim(col_slots, col_here, 0, keepdims=False)
    return (block_out, d_tokens, d_qkv, d_out_proj, d_up, d_down, small_rows, d_up_bias)


def shards(
    tokens,
    cotangent,
    timestep,
    piece_starts,
    w_mod,
    b_mod,
    gain_attn,
    w_qkv,
    w_out,
    gain_mlp,
    w_up,
    b_up,
    w_down,
    b_down,
):
    condition = embed_time(timestep[0].astype(jnp.float32))
    modulation = (
        jnp.einsum("k,kjd->jd", condition, w_mod.astype(jnp.float32), precision=precise) + b_mod
    )
    starts = piece_starts[0]
    results = blocked_layer(
        tokens,
        cotangent,
        modulation,
        starts,
        gain_attn,
        w_qkv,
        w_out,
        gain_mlp,
        w_up,
        b_up,
        w_down,
        b_down,
    )
    block_out, d_tokens, d_qkv, d_out_proj, d_up, d_down, small_rows, d_up_bias = results
    d_mod_w = condition[:, None, None] * small_rows[:6][None, :, :]
    d_qkv, d_out_proj, d_up, d_down, d_mod_w, small_rows, d_up_bias = lax.psum(
        (d_qkv, d_out_proj, d_up, d_down, d_mod_w, small_rows, d_up_bias), "dp"
    )
    return (
        block_out,
        d_tokens,
        d_mod_w,
        small_rows[:6],
        small_rows[6],
        d_qkv,
        d_out_proj,
        small_rows[7],
        d_up,
        d_up_bias,
        d_down,
        small_rows[8],
    )


def solution(mesh):
    return jax.shard_map(
        shards,
        mesh=mesh,
        in_specs=(
            P(("dp", "col"), "row"),
            P(("dp", "col"), "row"),
            P("dp"),
            P("dp", None),
            P(None, None, "row"),
            P(None, "row"),
            P("row"),
            P("col", "row"),
            P("col", "row"),
            P("row"),
            P("row", "col"),
            P("col"),
            P("col", "row"),
            P("row"),
        ),
        out_specs=(
            P(("dp", "col"), "row"),
            P(("dp", "col"), "row"),
            P(None, None, "row"),
            P(None, "row"),
            P("row"),
            P("col", "row"),
            P("col", "row"),
            P("row"),
            P("row", "col"),
            P("col"),
            P("col", "row"),
            P("row"),
        ),
        check_vma=False,
    )
```

profile of v0, /device:TPU:0, one launch (start us, length us, event | category | flops | bytes accessed | tf_op | source)
XLA Modules:
  0.0 1633.3 jit_solution(5533274232627833205)
XLA Ops:
  19.4 51.9 %all-gather.10.cloned.1.call-done = bf16[3072,384]{1,0:T(8,128)(2,1)} async-done(((bf16[768,384]{1,0:T(8,128)(2,1)}), bf16[3072,384]{1,0:T(8,128)(2,1)}) %all-gather.10.cloned.1.call-update) | async-done | bytes 2359312 | tf_op jit(solution)/shard_map/all_gather | solution.py:56
  79.3 83.1 %reduce-scatter.10.cloned.1.call-done = f32[1536,576]{0,1:T(8,128)} async-done(((f32[3072,576]{0,1:T(8,128)}), f32[1536,576]{0,1:T(8,128)}) %reduce-scatter.10.cloned.1.call-update) | async-done | bytes 3538960 | tf_op jit(solution)/shard_map/reduce_scatter | solution.py:65
  172.0 31.4 %all-gather.12.cloned.1.call-done = bf16[3072,384]{0,1:T(8,128)(2,1)} async-done(((bf16[1536,384]{0,1:T(8,128)(2,1)}), bf16[3072,384]{0,1:T(8,128)(2,1)}) %all-gather.12.cloned.1.call-update) | async-done | bytes 2359312 | tf_op jit(solution)/shard_map/all_gather | solution.py:261
  213.1 93.5 %while.30 = (s32[]{:T(128)}, bf16[3,1536,64]{1,2,0:T(8,128)(2,1)S(1)}, f32[3,1536]{1,0:T(4,128)}, bf16[3,1536,64]{2,1,0:T(8,128)(2,1)}, bf16[3,3072,64]{2,1,0:T(...) while((s32[]{:T(128)}, ...), condition=%wide.region_10.11_spmd.clone.clone, body=%wide.region_7.10_spmd.clone.sunk.clone | while | flops 1264581120 | bytes 59093104 | solution.py:171
  213.1 12.4 fusion.165
  244.3 12.3 fusion.165
  275.5 12.3 fusion.165
  307.6 22.9 %all-gather.14.cloned.1.call-done = bf16[3072,192]{0,1:T(8,128)(2,1)} async-done(((bf16[1536,192]{0,1:T(8,128)(2,1)}), bf16[3072,192]{0,1:T(8,128)(2,1)}) %all-gather.14.cloned.1.call-update) | async-done | bytes 1179664 | tf_op jit(solution)/shard_map/all_gather | solution.py:76
  337.5 82.8 %reduce-scatter.12.cloned.1.call-done = f32[768,384]{1,0:T(8,128)} async-done(((f32[3072,384]{1,0:T(8,128)}), f32[768,384]{1,0:T(8,128)}) %reduce-scatter.12.cloned.1.call-update) | async-done | bytes 1179664 | tf_op jit(solution)/shard_map/reduce_scatter | solution.py:85
  428.4 44.5 %all-gather.20.cloned.1.call-done = bf16[3072,384]{1,0:T(8,128)(2,1)} async-done(((bf16[768,384]{1,0:T(8,128)(2,1)}), bf16[3072,384]{1,0:T(8,128)(2,1)}) %all-gather.20.cloned.1.call-update) | async-done | bytes 2359312 | tf_op jit(solution)/shard_map/all_gather | solution.py:56
  480.9 42.9 %all-gather.16.cloned.1.call-done = bf16[3072,384]{1,0:T(8,128)(2,1)} async-done(((bf16[768,384]{1,0:T(8,128)(2,1)}), bf16[3072,384]{1,0:T(8,128)(2,1)}) %all-gather.16.cloned.1.call-update) | async-done | bytes 2359312 | tf_op jit(solution)/shard_map/all_gather | solution.py:56
  532.6 102.9 %reduce-scatter.18.cloned.1.call-done = f32[1536,768]{1,0:T(8,128)} async-done(((f32[3072,768]{1,0:T(8,128)}), f32[1536,768]{1,0:T(8,128)}) %reduce-scatter.18.cloned.1.call-update) | async-done | bytes 4718608 | tf_op jit(solution)/shard_map/reduce_scatter | solution.py:65
  635.5 113.0 %reduce-scatter.14.cloned.1.call-done = f32[1536,768]{1,0:T(8,128)} async-done(((f32[3072,768]{1,0:T(8,128)}), f32[1536,768]{1,0:T(8,128)}) %reduce-scatter.14.cloned.1.call-update) | async-done | bytes 4718608 | tf_op jit(solution)/shard_map/reduce_scatter | solution.py:65
  757.7 62.0 %all-gather.22.cloned.1.call-done = bf16[3072,768]{1,0:T(8,128)(2,1)} async-done(((bf16[1536,768]{1,0:T(8,128)(2,1)}), bf16[3072,768]{1,0:T(8,128)(2,1)}) %all-gather.22.cloned.1.call-update) | async-done | bytes 4718608 | tf_op jit(solution)/shard_map/all_gather | solution.py:76
  826.8 57.0 %all-gather.18.cloned.1.call-done = bf16[3072,768]{1,0:T(8,128)(2,1)} async-done(((bf16[1536,768]{1,0:T(8,128)(2,1)}), bf16[3072,768]{1,0:T(8,128)(2,1)}) %all-gather.18.cloned.1.call-update) | async-done | bytes 4718608 | tf_op jit(solution)/shard_map/all_gather | solution.py:76
  891.5 79.8 %reduce-scatter.20.cloned.1.call-done = f32[768,384]{1,0:T(8,128)} async-done(((f32[3072,384]{1,0:T(8,128)}), f32[768,384]{1,0:T(8,128)}) %reduce-scatter.20.cloned.1.call-update) | async-done | bytes 1179664 | tf_op jit(solution)/shard_map/reduce_scatter | solution.py:85
  978.9 80.6 %reduce-scatter.16.cloned.1.call-done = f32[768,384]{1,0:T(8,128)} async-done(((f32[3072,384]{1,0:T(8,128)}), f32[768,384]{1,0:T(8,128)}) %reduce-scatter.16.cloned.1.call-update) | async-done | bytes 1179664 | tf_op jit(solution)/shard_map/reduce_scatter | solution.py:85
  1065.0 50.6 %all-gather.24.cloned.1.call-done = bf16[3072,384]{1,0:T(8,128)(2,1)} async-done(((bf16[768,384]{1,0:T(8,128)(2,1)}), bf16[3072,384]{1,0:T(8,128)(2,1)}) %all-gather.24.cloned.1.call-update) | async-done | bytes 2359312 | tf_op jit(solution)/shard_map/all_gather | solution.py:56
  1119.8 33.6 %reduce-scatter.22.cloned.1.call-done = f32[1536,192]{0,1:T(8,128)} async-done(((f32[3072,192]{0,1:T(8,128)}), f32[1536,192]{0,1:T(8,128)}) %reduce-scatter.22.cloned.1.call-update) | async-done | bytes 1179664 | tf_op jit(solution)/shard_map/reduce_scatter | solution.py:65
  1156.0 147.2 %while.31 = (s32[]{:T(128)}, f32[3,1536,64]{1,2,0:T(8,128)}, bf16[3,3072,64]{1,2,0:T(8,128)(2,1)}, bf16[3,3072,64]{1,2,0:T(8,128)(2,1)}, bf16[3,1536,64]{2,1,0:T...) while((s32[]{:T(128)}, f32[3,1536,64]{1,2,0:T(8,128)}, ...), condition=%wide.region_27.28_spmd.clone.clone, body=%wide.region_25.27_spmd.clone.sunk.clone | while | flops 3081533952 | bytes 189987504 | solution.py:191
  1165.9 13.4 multiply_reduce_fusion.10
  1179.3 13.0 multiply_convert_fusion.5
  1215.0 13.4 multiply_reduce_fusion.10
  1228.4 13.0 multiply_convert_fusion.5
  1264.0 13.4 multiply_reduce_fusion.10
  1277.4 13.0 multiply_convert_fusion.5
  1306.7 34.7 %reduce-scatter.24.cloned.1.call-done = bf16[1536,384]{0,1:T(8,128)(2,1)} async-done(((bf16[3072,384]{0,1:T(8,128)(2,1)}), bf16[1536,384]{0,1:T(8,128)(2,1)}) %reduce-scatter.24.cloned.1.call-update) | async-done | bytes 1179664 | tf_op jit(solution)/shard_map/reduce_scatter | solution.py:298
  1345.5 49.4 %all-gather.26.cloned.1.call-done = bf16[3072,576]{0,1:T(8,128)(2,1)} async-done(((bf16[1536,576]{0,1:T(8,128)(2,1)}), bf16[3072,576]{0,1:T(8,128)(2,1)}) %all-gather.26.cloned.1.call-update) | async-done | bytes 3538960 | tf_op jit(solution)/shard_map/all_gather | solution.py:76
  1419.7 67.3 %reduce-scatter.26.cloned.1.call-done = f32[768,384]{1,0:T(8,128)} async-done(((f32[3072,384]{1,0:T(8,128)}), f32[768,384]{1,0:T(8,128)}) %reduce-scatter.26.cloned.1.call-update) | async-done | bytes 1179664 | tf_op jit(solution)/shard_map/reduce_scatter | solution.py:85
  1489.3 37.4 %all-reduce.4 = (f32[2,9,384]{2,1,0:T(8,128)S(1)}, f32[4,768]{1,0:T(4,128)S(1)}) all-reduce(f32[2,9,384]{2,1,0:T(8,128)S(1)} %broadcast_select_fusion, f32[4,768]{1,0:T(4,128)S(1)} %broadcast_select_fusion.1), channel_id=1, replica_groups=mesh['dp'=4,'row'=2,'col'=4] {'row','col'}, use_global_device_ids=true, to_apply=%region_43.44 | all-reduce | flops 9984 | bytes 79872 | tf_op jit(solution)/shard_map/psum | solution.py:337
  1528.0 11.9 all-reduce.5
  1547.6 72.0 %all-reduce.13.cloned.1.call-done = (f32[128,6,384]{2,0,1:T(8,128)}, f32[576,384]{1,0:T(8,128)}, f32[192,384]{1,0:T(8,128)}, f32[384,768]{1,0:T(8,128)}, f32[768,384]{1,0:T(8,128)}) async-done(((f32[128,6,384]{2,0,1:T(8,128)}, f32[576,384]{1,0:T(8,128)}, f32[192,384]{1,0:T(8,128)}, f32[384,768]{1,0:T(8,128)}, f32[768,384]{1,0:T(8,128)}), (f32[128,6,384]{2,0,1:T(8,128)}, f32[576,384]{1,0:T(8,128)}, ...) | async-done | bytes 4718608 | tf_op jit(solution)/shard_map/psum | solution.py:380
  (298 shorter events, 289.5 us)
Async XLA Ops:
  7.2 516.6 %copy-start = (bf16[384,768]{1,0:T(8,128)(2,1)S(1)}, bf16[384,768]{1,0:T(8,128)(2,1)}, u32[]{:S(2)}) copy-start(bf16[384,768]{1,0:T(8,128)(2,1)} %param.28) | copy-start | bytes 1769476
  7.2 64.0 %all-gather.10.cloned.1.call-start = ((), (), s32[]{:S(2)}) async-start(), calls=%async_computation.9 | async-start | bytes 2949120 | tf_op jit(solution)/shard_map/all_gather | solution.py:56
  19.3 143.2 %reduce-scatter.10.cloned.1.call-start = ((), (), s32[]{:S(2)}) async-start(), calls=%async_computation.10 | async-start | bytes 10616832 | tf_op jit(solution)/shard_map/reduce_scatter | solution.py:65
  77.9 125.5 %all-gather.12.cloned.1.call-start = ((), (), s32[]{:S(2)}) async-start(), calls=%async_computation.11 | async-start | bytes 3538944 | tf_op jit(solution)/shard_map/all_gather | solution.py:261
  79.3 86.3 %copy-start.20 = (f32[1536,32]{0,1:T(8,128)}, f32[1536,32]{0,1:T(8,128)S(1)}, u32[]{:S(2)}) copy-start(f32[1536,32]{0,1:T(8,128)S(1)} %get-tuple-element.356) | copy-start | bytes 589828
  79.3 86.3 %copy-start.22 = (f32[1536,32]{0,1:T(8,128)}, f32[1536,32]{0,1:T(8,128)S(1)}, u32[]{:S(2)}) copy-start(f32[1536,32]{0,1:T(8,128)S(1)} %get-tuple-element.357) | copy-start | bytes 589828
  167.2 163.3 %all-gather.14.cloned.1.call-start = ((), (), s32[]{:S(2)}) async-start(), calls=%async_computation.12 | async-start | bytes 1769472 | tf_op jit(solution)/shard_map/all_gather | solution.py:76
  307.5 112.8 %reduce-scatter.12.cloned.1.call-start = ((), (), s32[]{:S(2)}) async-start(), calls=%async_computation.13 | async-start | bytes 5898240 | tf_op jit(solution)/shard_map/reduce_scatter | solution.py:85
  334.9 85.4 %copy-start.7 = (bf16[768,384]{1,0:T(8,128)(2,1)S(1)}, bf16[768,384]{1,0:T(8,128)(2,1)}, u32[]{:S(2)}) copy-start(bf16[768,384]{1,0:T(8,128)(2,1)} %param.18) | copy-start | bytes 1769476
  334.9 85.4 %copy-start.42 = (f32[384]{0:T(512)S(1)}, f32[384]{0:T(512)}, u32[]{:S(2)}) copy-start(f32[384]{0:T(512)} %get-tuple-element.258) | copy-start | bytes 4612
  334.9 138.0 %all-gather.20.cloned.1.call-start = ((), (), s32[]{:S(2)}) async-start(), calls=%async_computation.18 | async-start | bytes 2949120 | tf_op jit(solution)/shard_map/all_gather | solution.py:56
  337.5 186.3 %all-gather.16.cloned.1.call-start = ((), (), s32[]{:S(2)}) async-start(), calls=%async_computation.14 | async-start | bytes 2949120 | tf_op jit(solution)/shard_map/all_gather | solution.py:56
  428.1 207.4 %reduce-scatter.18.cloned.1.call-start = ((), (), s32[]{:S(2)}) async-start(), calls=%async_computation.19 | async-start | bytes 14155776 | tf_op jit(solution)/shard_map/reduce_scatter | solution.py:65
  480.8 267.7 %reduce-scatter.14.cloned.1.call-start = ((), (), s32[]{:S(2)}) async-start(), calls=%async_computation.15 | async-start | bytes 14155776 | tf_op jit(solution)/shard_map/reduce_scatter | solution.py:65
  532.0 287.7 %all-gather.22.cloned.1.call-start = ((), (), s32[]{:S(2)}) async-start(), calls=%async_computation.20 | async-start | bytes 7077888 | tf_op jit(solution)/shard_map/all_gather | solution.py:76
  756.9 127.0 %all-gather.18.cloned.1.call-start = ((), (), s32[]{:S(2)}) async-start(), calls=%async_computation.16 | async-start | bytes 7077888 | tf_op jit(solution)/shard_map/all_gather | solution.py:76
  757.6 213.7 %reduce-scatter.20.cloned.1.call-start = ((), (), s32[]{:S(2)}) async-start(), calls=%async_computation.21 | async-start | bytes 5898240 | tf_op jit(solution)/shard_map/reduce_scatter | solution.py:85
  826.8 232.7 %reduce-scatter.16.cloned.1.call-start = ((), (), s32[]{:S(2)}) async-start(), calls=%async_computation.17 | async-start | bytes 5898240 | tf_op jit(solution)/shard_map/reduce_scatter | solution.py:85
  891.0 80.4 %copy-start.46 = (f32[384]{0:T(512)S(1)}, f32[384]{0:T(512)}, u32[]{:S(2)}) copy-start(f32[384]{0:T(512)} %param.27) | copy-start | bytes 4612
  891.0 168.5 %copy-start.15 = (f32[768,384]{1,0:T(8,128)S(1)}, f32[768,384]{1,0:T(8,128)}, u32[]{:S(2)}) copy-start(f32[768,384]{1,0:T(8,128)} %reduce-scatter.12.cloned.1.call-done) | copy-start | bytes 3538948
  891.0 168.5 %copy-start.44 = (f32[384]{0:T(512)S(1)}, f32[384]{0:T(512)}, u32[]{:S(2)}) copy-start(f32[384]{0:T(512)} %get-tuple-element.253) | copy-start | bytes 4612
  891.0 168.5 %copy-start.61 = (f32[384]{0:T(512)S(1)}, f32[384]{0:T(512)}, u32[]{:S(2)}) copy-start(f32[384]{0:T(512)} %param.31) | copy-start | bytes 4612
  891.0 224.6 %all-gather.24.cloned.1.call-start = ((), (), s32[]{:S(2)}) async-start(), calls=%async_computation.22 | async-start | bytes 2949120 | tf_op jit(solution)/shard_map/all_gather | solution.py:56
  1064.9 88.5 %reduce-scatter.22.cloned.1.call-start = ((), (), s32[]{:S(2)}) async-start(), calls=%async_computation.23 | async-start | bytes 3538944 | tf_op jit(solution)/shard_map/reduce_scatter | solution.py:65
  1119.7 221.8 %reduce-scatter.24.cloned.1.call-start = ((), (), s32[]{:S(2)}) async-start(), calls=%async_computation.24 | async-start | bytes 3538944 | tf_op jit(solution)/shard_map/reduce_scatter | solution.py:298
  1306.5 88.5 %all-gather.26.cloned.1.call-start = ((), (), s32[]{:S(2)}) async-start(), calls=%async_computation.25 | async-start | bytes 5308416 | tf_op jit(solution)/shard_map/all_gather | solution.py:76
  1345.5 141.6 %reduce-scatter.26.cloned.1.call-start = ((), (), s32[]{:S(2)}) async-start(), calls=%async_computation.26 | async-start | bytes 5898240 | tf_op jit(solution)/shard_map/reduce_scatter | solution.py:85
  1401.6 218.0 %all-reduce.13.cloned.1.call-start = ((), (), s32[]{:S(2)}) async-start(), calls=%async_computation.27 | async-start | bytes 9437184 | tf_op jit(solution)/shard_map/psum | solution.py:380
  1416.8 70.3 %copy-start.36 = (f32[768]{0:T(1024)S(1)}, f32[768]{0:T(1024)}, u32[]{:S(2)}) copy-start(f32[768]{0:T(1024)} %copy-done.35) | copy-start | bytes 9220
  1416.8 70.3 %copy-start.38 = (f32[384]{0:T(512)S(1)}, f32[384]{0:T(512)}, u32[]{:S(2)}) copy-start(f32[384]{0:T(512)} %copy-done.37) | copy-start | bytes 4612
  1416.8 70.3 %copy-start.41 = (f32[384]{0:T(512)S(1)}, f32[384]{0:T(512)}, u32[]{:S(2)}) copy-start(f32[384]{0:T(512)} %param.24) | copy-start | bytes 4612
  1419.7 107.0 %copy-start.60 = (f32[128]{0:T(128)S(1)}, f32[128]{0:T(128)}, u32[]{:S(2)}) copy-start(f32[128]{0:T(128)} %copy-done.59) | copy-start | bytes 1540
  (54 other events, 659.3 us)
Sparse Core Ops, SparseCore 0:
  19.4 51.7 all-gather.9
  78.0 84.4 reduce-scatter.9
  167.3 36.0 all-gather.11
  307.6 22.7 all-gather.13
  335.0 85.2 reduce-scatter.11
  422.3 50.5 all-gather.19
  475.0 48.7 all-gather.15
  526.1 109.3 reduce-scatter.17
  637.8 110.6 reduce-scatter.13
  757.0 62.6 all-gather.21
  821.2 62.6 all-gather.17
  886.0 85.2 reduce-scatter.19
  973.6 85.7 reduce-scatter.15
  1065.0 50.5 all-gather.23
  1119.8 33.5 reduce-scatter.21
  1306.6 34.7 reduce-scatter.23
  1345.6 49.3 all-gather.25
  1401.7 85.2 reduce-scatter.25
  1528.0 91.4 all-reduce.12
where the time goes:
time: 1640 us; the launch traced here: 1630 us
  waiting for transfers between devices  1160 us (71%)
  matrix products  238 us (15%)
  other arithmetic  106 us (6%)
  blocking collectives  70.1 us (4%)
  local copies, waits for them, and re-layouts  38.3 us (2%)
    reduce_scatter x4, waiting for transfers between devices, into_heads(): lax.psum_scatter(partial_product(jnp.int32(0), share_rows * lax.axis_size...  333 us
    reduce_scatter x4, waiting for transfers between devices, into_stream(): lax.psum_scatter(partial_product(jnp.int32(0), share_rows * lax.axis_size...  311 us
    all_gather x4, waiting for transfers between devices, into_stream(): gathered = lax.all_gather(activation, 'row', axis=0, tiled=True)  191 us
    all_gather x4, waiting for transfers between devices, into_heads(): gathered = lax.all_gather(activation, 'col', axis=0, tiled=True)  190 us
    psum x1, waiting for transfers between devices, shards(): lax.psum((d_qkv, d_out_proj, d_up, d_down, d_mod_w, small_rows, d_up_bias...  72 us
    dot_general x8, matrix products, partial_product(): lax.dot_general(gathered, weight, (((1,), (contract,)), ((), ())), prefer...  52 us
    dot_general x10, matrix products, weight_grad(): lax.dot_general(first_operand, second_operand, (((0,), (0,)), ((), ())),...  43 us
    dot_general x3, matrix products, attend_back(): lax.dot_general(query_head, key_head, (((1,), (1,)), ((), ())), preferred...  40.2 us
  transfers between devices with their start and end apart: 19, of which 19 were waited for; matrix products, arithmetic and copies ran while one was open for 4% of the time, Pallas kernels for 0%

commit v1 on v0

--- a/solution.py
+++ b/solution.py
@@ -3,6 +3,7 @@
 import jax.numpy as jnp
 from jax import lax
 from jax.sharding import PartitionSpec as P
+from jax.lax import axis_index, axis_size, ppermute
 
 D = 768
 HEAD = 64
@@ -11,6 +12,40 @@
 PIECES = 4
 precise = lax.Precision.HIGHEST
 epsilon = 1e-05
+
+
+def roots_check(patch, dim_k):
+    r2 = list(patch.shape[1:])
+    r2[dim_k] *= patch.shape[0]
+    return jnp.moveaxis(patch, 0, dim_k).reshape(r2)
+
+
+def map_remake(u_in, chip_axis, dim_at):
+    count_all = axis_size(chip_axis)
+    panels = []
+    to_i = 0
+    while to_i < count_all:
+        panels.append((to_i, (to_i + 1) % count_all))
+        to_i += 1
+    kept_rows = []
+    for u, b in panels:
+        kept_rows.append((b, u))
+    part_now, x_new = ([], [])
+    dev_i = 0
+    while dev_i < count_all - 1:
+        if dev_i % 2 == 0:
+            e_next = ppermute(part_now[-1] if part_now else u_in, chip_axis, panels)
+            part_now.append(e_next)
+        else:
+            x_next = ppermute(x_new[-1] if x_new else u_in, chip_axis, kept_rows)
+            x_new.append(x_next)
+        dev_i = dev_i + 1
+    reply = jnp.stack([*part_now[::-1], u_in, *x_new])
+    carry_out = axis_index(chip_axis)
+    found_now = len(part_now)
+    arr_now = carry_out - found_now
+    reply = reply[(jnp.arange(count_all) - arr_now) % count_all]
+    return roots_check(reply, dim_at)
 
 
 def embed_time(time_step):
@@ -53,7 +88,7 @@
 
 
 def into_heads(activation, weight, contract):
-    gathered = lax.all_gather(activation, "col", axis=0, tiled=True)
+    gathered = map_remake(activation, "col", 0)
     share_rows = gathered.shape[0] // lax.axis_size("row")
 
     def partial_product(start_row, row_count):

time: 1640 us -> 1560 us (0.951)
  waiting for transfers between devices: 1160 us -> 1020 us
  starting transfers between devices: 1.75 us -> 55 us
    all_gather x4 -> x0, waiting for transfers between devices: 190 us -> none  [into_heads(): gathered = lax.all_gather(activation, 'col', axis=0, tiled=True)]
    ppermute x0 -> x12, waiting for transfers between devices: none -> 146 us  [the longest x8 123 us: map_remake(): e_next = ppermute(part_now[-1] if part_now else u_in, chip_axis, panels)]
    ppermute x0 -> x12, starting transfers between devices: none -> 53.8 us  [the longest x8 44.3 us: map_remake(): e_next = ppermute(part_now[-1] if part_now else u_in, chip_axis, panels)]
    reduce_scatter x4, waiting for transfers between devices: 311 us -> 258 us  [into_stream(): lax.psum_scatter(partial_product(jnp.int32(0), share_rows * lax.axis_size...]
    reduce_scatter x4, waiting for transfers between devices: 333 us -> 283 us  [into_heads(): lax.psum_scatter(partial_product(jnp.int32(0), share_rows * lax.axis_size...]
  transfers between devices with their start and end apart: 19 -> 27, of which waited for: 19 -> 27; matrix products, arithmetic and copies ran while one was open for 4% -> 4% of each run, Pallas kernels for 0% -> 0%
where the time goes in v1:
time: 1560 us; the launch traced here: 1550 us
  waiting for transfers between devices  1020 us (65%)
  matrix products  230 us (15%)
  other arithmetic  115 us (7%)
  blocking collectives  70.1 us (4%)
  starting transfers between devices  55 us (4%)
  local copies, waits for them, and re-layouts  46.8 us (3%)
  between operations  15.8 us (1%)
    reduce_scatter x4, waiting for transfers between devices, into_heads(): lax.psum_scatter(partial_product(jnp.int32(0), share_rows * lax.axis_size...  283 us
    reduce_scatter x4, waiting for transfers between devices, into_stream(): lax.psum_scatter(partial_product(jnp.int32(0), share_rows * lax.axis_size...  258 us
    all_gather x4, waiting for transfers between devices, into_stream(): gathered = lax.all_gather(activation, 'row', axis=0, tiled=True)  191 us
    ppermute x8, waiting for transfers between devices, map_remake(): e_next = ppermute(part_now[-1] if part_now else u_in, chip_axis, panels)  123 us
    psum x1, waiting for transfers between devices, shards(): lax.psum((d_qkv, d_out_proj, d_up, d_down, d_mod_w, small_rows, d_up_bias...  72 us
    ppermute x8, starting transfers between devices, map_remake(): e_next = ppermute(part_now[-1] if part_now else u_in, chip_axis, panels)  44.3 us
    dot_general x8, matrix products, partial_product(): lax.dot_general(gathered, weight, (((1,), (contract,)), ((), ())), prefer...  44.3 us
    dot_general x10, matrix products, weight_grad(): lax.dot_general(first_operand, second_operand, (((0,), (0,)), ((), ())),...  42.9 us
  transfers between devices with their start and end apart: 27, of which 27 were waited for; matrix products, arithmetic and copies ran while one was open for 4% of the time, Pallas kernels for 0%

profile of v1, /device:TPU:0, one launch (start us, length us, event | category | flops | bytes accessed | tf_op | source)
XLA Modules:
  0.0 1550.5 jit_solution(10703771951746267699)
XLA Ops:
  24.4 14.1 collective-permute-done
  73.0 83.7 %reduce-scatter.10.cloned.1.call-done = f32[1536,576]{0,1:T(8,128)} async-done(((f32[3072,576]{0,1:T(8,128)}), f32[1536,576]{0,1:T(8,128)}) %reduce-scatter.10.cloned.1.call-update) | async-done | bytes 3538960 | tf_op jit(solution)/shard_map/reduce_scatter | solution.py:100
  165.8 31.8 %all-gather.6.cloned.1.call-done = bf16[3072,384]{0,1:T(8,128)(2,1)} async-done(((bf16[1536,384]{0,1:T(8,128)(2,1)}), bf16[3072,384]{0,1:T(8,128)(2,1)}) %all-gather.6.cloned.1.call-update) | async-done | bytes 2359312 | tf_op jit(solution)/shard_map/all_gather | solution.py:296
  207.4 93.6 %while.30 = (s32[]{:T(128)}, bf16[3,1536,64]{1,2,0:T(8,128)(2,1)S(1)}, f32[3,1536]{1,0:T(4,128)}, bf16[3,1536,64]{2,1,0:T(8,128)(2,1)}, bf16[3,3072,64]{2,1,0:T(...) while((s32[]{:T(128)}, ...), condition=%wide.region_10.11_spmd.clone.clone, body=%wide.region_7.10_spmd.clone.sunk.clone | while | flops 1264581120 | bytes 59093104 | solution.py:206
  207.4 12.4 fusion.170
  301.9 22.9 %all-gather.8.cloned.1.call-done = bf16[3072,192]{0,1:T(8,128)(2,1)} async-done(((bf16[1536,192]{0,1:T(8,128)(2,1)}), bf16[3072,192]{0,1:T(8,128)(2,1)}) %all-gather.8.cloned.1.call-update) | async-done | bytes 1179664 | tf_op jit(solution)/shard_map/all_gather | solution.py:111
  334.9 24.0 %collective-permute-done.6 = bf16[768,384]{1,0:T(8,128)(2,1)S(1)} collective-permute-done((bf16[768,384]{1,0:T(8,128)(2,1)S(1)}, bf16[768,384]{1,0:T(8,128)(2,1)S(1)}, u32[]{:S(2)}, u32[]{:S(2)}) %collective-permute-start.6) | collective-permute-done | bytes 589856 | tf_op jit(solution)/shard_map/ppermute | solution.py:37
  358.9 19.1 %collective-permute-start.7 = (bf16[768,384]{1,0:T(8,128)(2,1)S(1)}, bf16[768,384]{1,0:T(8,128)(2,1)S(1)}, u32[]{:S(2)}, u32[]{:S(2)}) collective-permute-start(bf16[768,384]{1,0:T(8,128)(2,1)S(1)} %collective-permute-done.6), channel_id=1, source_target_pairs={{0,1},{1,2},{2,3},{3,0},{4,5},{5,6},{6,7},{7,4},{8,9},{9,10},{10,1... | collective-permute-start | bytes 1769480 | tf_op jit(solution)/shard_map/ppermute | solution.py:37
  388.6 19.6 %collective-permute-done.7 = bf16[768,384]{1,0:T(8,128)(2,1)S(1)} collective-permute-done((bf16[768,384]{1,0:T(8,128)(2,1)S(1)}, bf16[768,384]{1,0:T(8,128)(2,1)S(1)}, u32[]{:S(2)}, u32[]{:S(2)}) %collective-permute-start.7) | collective-permute-done | bytes 589856 | tf_op jit(solution)/shard_map/ppermute | solution.py:37
  419.5 30.3 %reduce-scatter.12.cloned.1.call-done = f32[768,384]{1,0:T(8,128)} async-done(((f32[3072,384]{1,0:T(8,128)}), f32[768,384]{1,0:T(8,128)}) %reduce-scatter.12.cloned.1.call-update) | async-done | bytes 1179664 | tf_op jit(solution)/shard_map/reduce_scatter | solution.py:120
  460.6 14.2 collective-permute-done.3
  485.6 12.5 collective-permute-done.4
  508.6 53.0 %reduce-scatter.18.cloned.1.call-done = f32[1536,768]{1,0:T(8,128)} async-done(((f32[3072,768]{1,0:T(8,128)}), f32[1536,768]{1,0:T(8,128)}) %reduce-scatter.18.cloned.1.call-update) | async-done | bytes 4718608 | tf_op jit(solution)/shard_map/reduce_scatter | solution.py:100
  561.6 112.8 %reduce-scatter.14.cloned.1.call-done = f32[1536,768]{1,0:T(8,128)} async-done(((f32[3072,768]{1,0:T(8,128)}), f32[1536,768]{1,0:T(8,128)}) %reduce-scatter.14.cloned.1.call-update) | async-done | bytes 4718608 | tf_op jit(solution)/shard_map/reduce_scatter | solution.py:100
  683.6 62.0 %all-gather.12.cloned.1.call-done = bf16[3072,768]{1,0:T(8,128)(2,1)} async-done(((bf16[1536,768]{1,0:T(8,128)(2,1)}), bf16[3072,768]{1,0:T(8,128)(2,1)}) %all-gather.12.cloned.1.call-update) | async-done | bytes 4718608 | tf_op jit(solution)/shard_map/all_gather | solution.py:111
  753.0 56.8 %all-gather.10.cloned.1.call-done = bf16[3072,768]{1,0:T(8,128)(2,1)} async-done(((bf16[1536,768]{1,0:T(8,128)(2,1)}), bf16[3072,768]{1,0:T(8,128)(2,1)}) %all-gather.10.cloned.1.call-update) | async-done | bytes 4718608 | tf_op jit(solution)/shard_map/all_gather | solution.py:111
  817.1 80.4 %reduce-scatter.20.cloned.1.call-done = f32[768,384]{1,0:T(8,128)} async-done(((f32[3072,384]{1,0:T(8,128)}), f32[768,384]{1,0:T(8,128)}) %reduce-scatter.20.cloned.1.call-update) | async-done | bytes 1179664 | tf_op jit(solution)/shard_map/reduce_scatter | solution.py:120
  905.0 80.4 %reduce-scatter.16.cloned.1.call-done = f32[768,384]{1,0:T(8,128)} async-done(((f32[3072,384]{1,0:T(8,128)}), f32[768,384]{1,0:T(8,128)}) %reduce-scatter.16.cloned.1.call-update) | async-done | bytes 1179664 | tf_op jit(solution)/shard_map/reduce_scatter | solution.py:120
  992.9 14.2 collective-permute-done.9
  1038.4 34.0 %reduce-scatter.22.cloned.1.call-done = f32[1536,192]{0,1:T(8,128)} async-done(((f32[3072,192]{0,1:T(8,128)}), f32[1536,192]{0,1:T(8,128)}) %reduce-scatter.22.cloned.1.call-update) | async-done | bytes 1179664 | tf_op jit(solution)/shard_map/reduce_scatter | solution.py:100
  1074.5 147.2 %while.31 = (s32[]{:T(128)}, f32[3,1536,64]{1,2,0:T(8,128)}, bf16[3,3072,64]{1,2,0:T(8,128)(2,1)}, bf16[3,3072,64]{1,2,0:T(8,128)(2,1)}, bf16[3,1536,64]{2,1,0:T...) while((s32[]{:T(128)}, f32[3,1536,64]{1,2,0:T(8,128)}, ...), condition=%wide.region_27.28_spmd.clone.clone, body=%wide.region_25.27_spmd.clone.sunk.clone | while | flops 3081533952 | bytes 189987504 | solution.py:226
  1084.4 13.4 multiply_reduce_fusion.10
  1097.8 13.0 multiply_convert_fusion.5
  1133.5 13.4 multiply_reduce_fusion.10
  1146.9 13.0 multiply_convert_fusion.5
  1182.5 13.4 multiply_reduce_fusion.10
  1195.9 13.0 multiply_convert_fusion.5
  1225.1 34.9 %reduce-scatter.24.cloned.1.call-done = bf16[1536,384]{0,1:T(8,128)(2,1)} async-done(((bf16[3072,384]{0,1:T(8,128)(2,1)}), bf16[1536,384]{0,1:T(8,128)(2,1)}) %reduce-scatter.24.cloned.1.call-update) | async-done | bytes 1179664 | tf_op jit(solution)/shard_map/reduce_scatter | solution.py:333
  1263.7 49.2 %all-gather.14.cloned.1.call-done = bf16[3072,576]{0,1:T(8,128)(2,1)} async-done(((bf16[1536,576]{0,1:T(8,128)(2,1)}), bf16[3072,576]{0,1:T(8,128)(2,1)}) %all-gather.14.cloned.1.call-update) | async-done | bytes 3538960 | tf_op jit(solution)/shard_map/all_gather | solution.py:111
  1337.7 67.3 %reduce-scatter.26.cloned.1.call-done = f32[768,384]{1,0:T(8,128)} async-done(((f32[3072,384]{1,0:T(8,128)}), f32[768,384]{1,0:T(8,128)}) %reduce-scatter.26.cloned.1.call-update) | async-done | bytes 1179664 | tf_op jit(solution)/shard_map/reduce_scatter | solution.py:120
  1407.3 37.4 %all-reduce.4 = (f32[2,9,384]{2,1,0:T(8,128)S(1)}, f32[4,768]{1,0:T(4,128)S(1)}) all-reduce(f32[2,9,384]{2,1,0:T(8,128)S(1)} %broadcast_select_fusion, f32[4,768]{1,0:T(4,128)S(1)} %broadcast_select_fusion.1), channel_id=1, replica_groups=mesh['dp'=4,'row'=2,'col'=4] {'row','col'}, use_global_device_ids=true, to_apply=%region_43.44 | all-reduce | flops 9984 | bytes 79872 | tf_op jit(solution)/shard_map/psum | solution.py:372
  1465.5 72.0 %all-reduce.13.cloned.1.call-done = (f32[128,6,384]{2,0,1:T(8,128)}, f32[576,384]{1,0:T(8,128)}, f32[192,384]{1,0:T(8,128)}, f32[384,768]{1,0:T(8,128)}, f32[768,384]{1,0:T(8,128)}) async-done(((f32[128,6,384]{2,0,1:T(8,128)}, f32[576,384]{1,0:T(8,128)}, f32[192,384]{1,0:T(8,128)}, f32[384,768]{1,0:T(8,128)}, f32[768,384]{1,0:T(8,128)}), (f32[128,6,384]{2,0,1:T(8,128)}, f32[576,384]{1,0:T(8,128)}, ...) | async-done | bytes 4718608 | tf_op jit(solution)/shard_map/psum | solution.py:415
  (335 shorter events, 416.2 us)
Async XLA Ops:
  7.2 495.7 %copy-start = (bf16[384,768]{1,0:T(8,128)(2,1)S(1)}, bf16[384,768]{1,0:T(8,128)(2,1)}, u32[]{:S(2)}) copy-start(bf16[384,768]{1,0:T(8,128)(2,1)} %param.28) | copy-start | bytes 1769476
  7.2 149.5 %reduce-scatter.10.cloned.1.call-start = ((), (), s32[]{:S(2)}) async-start(), calls=%async_computation.9 | async-start | bytes 10616832 | tf_op jit(solution)/shard_map/reduce_scatter | solution.py:100
  20.2 18.4 %collective-permute-start = (bf16[768,384]{1,0:T(8,128)(2,1)S(1)}, bf16[768,384]{1,0:T(8,128)(2,1)S(1)}, u32[]{:S(2)}, u32[]{:S(2)}) collective-permute-start(bf16[768,384]{1,0:T(8,128)(2,1)S(1)} %fusion.66), channel_id=1, source_target_pairs={{0,1},{1,2},{2,3},{3,0},{4,5},{5,6},{6,7},{7,4},{8,9},{9,10},{10,1... | collective-permute-start | bytes 1769480 | tf_op jit(solution)/shard_map/ppermute | solution.py:37
  22.3 27.7 %collective-permute-start.2 = (bf16[768,384]{1,0:T(8,128)(2,1)S(1)}, bf16[768,384]{1,0:T(8,128)(2,1)S(1)}, u32[]{:S(2)}, u32[]{:S(2)}) collective-permute-start(bf16[768,384]{1,0:T(8,128)(2,1)S(1)} %fusion.66), channel_id=1, source_target_pairs={{1,0},{2,1},{3,2},{0,3},{5,4},{6,5},{7,6},{4,7},{9,8},{10,9},{11,1... | collective-permute-start | bytes 1769480 | tf_op jit(solution)/shard_map/ppermute | solution.py:40
  38.6 23.3 %collective-permute-start.1 = (bf16[768,384]{1,0:T(8,128)(2,1)S(1)}, bf16[768,384]{1,0:T(8,128)(2,1)S(1)}, u32[]{:S(2)}, u32[]{:S(2)}) collective-permute-start(bf16[768,384]{1,0:T(8,128)(2,1)S(1)} %collective-permute-done), channel_id=1, source_target_pairs={{0,1},{1,2},{2,3},{3,0},{4,5},{5,6},{6,7},{7,4},{8,9},{9,10},{10,1... | collective-permute-start | bytes 1769480 | tf_op jit(solution)/shard_map/ppermute | solution.py:37
  71.5 126.1 %all-gather.6.cloned.1.call-start = ((), (), s32[]{:S(2)}) async-start(), calls=%async_computation.10 | async-start | bytes 3538944 | tf_op jit(solution)/shard_map/all_gather | solution.py:296
  161.4 163.3 %all-gather.8.cloned.1.call-start = ((), (), s32[]{:S(2)}) async-start(), calls=%async_computation.11 | async-start | bytes 1769472 | tf_op jit(solution)/shard_map/all_gather | solution.py:111
  301.8 148.0 %reduce-scatter.12.cloned.1.call-start = ((), (), s32[]{:S(2)}) async-start(), calls=%async_computation.12 | async-start | bytes 5898240 | tf_op jit(solution)/shard_map/reduce_scatter | solution.py:120
  329.3 232.3 %reduce-scatter.18.cloned.1.call-start = ((), (), s32[]{:S(2)}) async-start(), calls=%async_computation.16 | async-start | bytes 14155776 | tf_op jit(solution)/shard_map/reduce_scatter | solution.py:100
  331.1 27.9 %collective-permute-start.6 = (bf16[768,384]{1,0:T(8,128)(2,1)S(1)}, bf16[768,384]{1,0:T(8,128)(2,1)S(1)}, u32[]{:S(2)}, u32[]{:S(2)}) collective-permute-start(bf16[768,384]{1,0:T(8,128)(2,1)S(1)} %get-tuple-element.325), channel_id=1, source_target_pairs={{0,1},{1,2},{2,3},{3,0},{4,5},{5,6},{6,7},{7,4},{8,9},{9,10},{10,1... | collective-permute-start | bytes 1769480 | tf_op jit(solution)/shard_map/ppermute | solution.py:37
  332.6 56.0 %collective-permute-start.8 = (bf16[768,384]{1,0:T(8,128)(2,1)S(1)}, bf16[768,384]{1,0:T(8,128)(2,1)S(1)}, u32[]{:S(2)}, u32[]{:S(2)}) collective-permute-start(bf16[768,384]{1,0:T(8,128)(2,1)S(1)} %get-tuple-element.325), channel_id=1, source_target_pairs={{1,0},{2,1},{3,2},{0,3},{5,4},{6,5},{7,6},{4,7},{9,8},{10,9},{11,1... | collective-permute-start | bytes 1769480 | tf_op jit(solution)/shard_map/ppermute | solution.py:40
  358.9 49.3 %collective-permute-start.7 = (bf16[768,384]{1,0:T(8,128)(2,1)S(1)}, bf16[768,384]{1,0:T(8,128)(2,1)S(1)}, u32[]{:S(2)}, u32[]{:S(2)}) collective-permute-start(bf16[768,384]{1,0:T(8,128)(2,1)S(1)} %collective-permute-done.6), channel_id=1, source_target_pairs={{0,1},{1,2},{2,3},{3,0},{4,5},{5,6},{6,7},{7,4},{8,9},{9,10},{10,1... | collective-permute-start | bytes 1769480 | tf_op jit(solution)/shard_map/ppermute | solution.py:37
  419.5 254.9 %reduce-scatter.14.cloned.1.call-start = ((), (), s32[]{:S(2)}) async-start(), calls=%async_computation.13 | async-start | bytes 14155776 | tf_op jit(solution)/shard_map/reduce_scatter | solution.py:100
  456.8 18.1 %collective-permute-start.3 = (bf16[768,384]{1,0:T(8,128)(2,1)S(1)}, bf16[768,384]{1,0:T(8,128)(2,1)S(1)}, u32[]{:S(2)}, u32[]{:S(2)}) collective-permute-start(bf16[768,384]{1,0:T(8,128)(2,1)S(1)} %add_convert_fusion.3), channel_id=1, source_target_pairs={{0,1},{1,2},{2,3},{3,0},{4,5},{5,6},{6,7},{7,4},{8,9},{9,10},{10,1... | collective-permute-start | bytes 1769480 | tf_op jit(solution)/shard_map/ppermute | solution.py:37
  458.0 27.6 %collective-permute-start.5 = (bf16[768,384]{1,0:T(8,128)(2,1)S(1)}, bf16[768,384]{1,0:T(8,128)(2,1)S(1)}, u32[]{:S(2)}, u32[]{:S(2)}) collective-permute-start(bf16[768,384]{1,0:T(8,128)(2,1)S(1)} %add_convert_fusion.3), channel_id=1, source_target_pairs={{1,0},{2,1},{3,2},{0,3},{5,4},{6,5},{7,6},{4,7},{9,8},{10,9},{11,1... | collective-permute-start | bytes 1769480 | tf_op jit(solution)/shard_map/ppermute | solution.py:40
  474.8 23.3 %collective-permute-start.4 = (bf16[768,384]{1,0:T(8,128)(2,1)S(1)}, bf16[768,384]{1,0:T(8,128)(2,1)S(1)}, u32[]{:S(2)}, u32[]{:S(2)}) collective-permute-start(bf16[768,384]{1,0:T(8,128)(2,1)S(1)} %collective-permute-done.3), channel_id=1, source_target_pairs={{0,1},{1,2},{2,3},{3,0},{4,5},{5,6},{6,7},{7,4},{8,9},{9,10},{10,1... | collective-permute-start | bytes 1769480 | tf_op jit(solution)/shard_map/ppermute | solution.py:37
  507.9 237.7 %all-gather.12.cloned.1.call-start = ((), (), s32[]{:S(2)}) async-start(), calls=%async_computation.17 | async-start | bytes 7077888 | tf_op jit(solution)/shard_map/all_gather | solution.py:111
  682.8 127.0 %all-gather.10.cloned.1.call-start = ((), (), s32[]{:S(2)}) async-start(), calls=%async_computation.14 | async-start | bytes 7077888 | tf_op jit(solution)/shard_map/all_gather | solution.py:111
  683.6 213.9 %reduce-scatter.20.cloned.1.call-start = ((), (), s32[]{:S(2)}) async-start(), calls=%async_computation.18 | async-start | bytes 5898240 | tf_op jit(solution)/shard_map/reduce_scatter | solution.py:120
  752.8 232.7 %reduce-scatter.16.cloned.1.call-start = ((), (), s32[]{:S(2)}) async-start(), calls=%async_computation.15 | async-start | bytes 5898240 | tf_op jit(solution)/shard_map/reduce_scatter | solution.py:120
  817.0 168.5 %copy-start.22 = (f32[768,384]{1,0:T(8,128)S(1)}, f32[768,384]{1,0:T(8,128)}, u32[]{:S(2)}) copy-start(f32[768,384]{1,0:T(8,128)} %reduce-scatter.12.cloned.1.call-done) | copy-start | bytes 3538948
  817.0 168.5 %copy-start.54 = (f32[384]{0:T(512)S(1)}, f32[384]{0:T(512)}, u32[]{:S(2)}) copy-start(f32[384]{0:T(512)} %get-tuple-element.253) | copy-start | bytes 4612
  817.0 168.5 %copy-start.67 = (f32[384]{0:T(512)S(1)}, f32[384]{0:T(512)}, u32[]{:S(2)}) copy-start(f32[384]{0:T(512)} %param.31) | copy-start | bytes 4612
  817.0 255.4 %reduce-scatter.22.cloned.1.call-start = ((), (), s32[]{:S(2)}) async-start(), calls=%async_computation.19 | async-start | bytes 3538944 | tf_op jit(solution)/shard_map/reduce_scatter | solution.py:100
  989.0 18.1 %collective-permute-start.9 = (bf16[768,384]{1,0:T(8,128)(2,1)S(1)}, bf16[768,384]{1,0:T(8,128)(2,1)S(1)}, u32[]{:S(2)}, u32[]{:S(2)}) collective-permute-start(bf16[768,384]{1,0:T(8,128)(2,1)S(1)} %multiply_convert_fusion.2), channel_id=1, source_target_pairs={{0,1},{1,2},{2,3},{3,0},{4,5},{5,6},{6,7},{7,4},{8,9},{9,10},{10,1... | collective-permute-start | bytes 1769480 | tf_op jit(solution)/shard_map/ppermute | solution.py:37
  990.6 28.5 %collective-permute-start.11 = (bf16[768,384]{1,0:T(8,128)(2,1)S(1)}, bf16[768,384]{1,0:T(8,128)(2,1)S(1)}, u32[]{:S(2)}, u32[]{:S(2)}) collective-permute-start(bf16[768,384]{1,0:T(8,128)(2,1)S(1)} %multiply_convert_fusion.2), channel_id=1, source_target_pairs={{1,0},{2,1},{3,2},{0,3},{5,4},{6,5},{7,6},{4,7},{9,8},{10,9},{11,1... | collective-permute-start | bytes 1769480 | tf_op jit(solution)/shard_map/ppermute | solution.py:40
  1007.1 24.1 %collective-permute-start.10 = (bf16[768,384]{1,0:T(8,128)(2,1)S(1)}, bf16[768,384]{1,0:T(8,128)(2,1)S(1)}, u32[]{:S(2)}, u32[]{:S(2)}) collective-permute-start(bf16[768,384]{1,0:T(8,128)(2,1)S(1)} %collective-permute-done.9), channel_id=1, source_target_pairs={{0,1},{1,2},{2,3},{3,0},{4,5},{5,6},{6,7},{7,4},{8,9},{9,10},{10,1... | collective-permute-start | bytes 1769480 | tf_op jit(solution)/shard_map/ppermute | solution.py:37
  1038.3 221.6 %reduce-scatter.24.cloned.1.call-start = ((), (), s32[]{:S(2)}) async-start(), calls=%async_computation.20 | async-start | bytes 3538944 | tf_op jit(solution)/shard_map/reduce_scatter | solution.py:333
  1225.0 87.9 %all-gather.14.cloned.1.call-start = ((), (), s32[]{:S(2)}) async-start(), calls=%async_computation.21 | async-start | bytes 5308416 | tf_op jit(solution)/shard_map/all_gather | solution.py:111
  1263.4 141.6 %reduce-scatter.26.cloned.1.call-start = ((), (), s32[]{:S(2)}) async-start(), calls=%async_computation.22 | async-start | bytes 5898240 | tf_op jit(solution)/shard_map/reduce_scatter | solution.py:120
  1319.6 218.0 %all-reduce.13.cloned.1.call-start = ((), (), s32[]{:S(2)}) async-start(), calls=%async_computation.23 | async-start | bytes 9437184 | tf_op jit(solution)/shard_map/psum | solution.py:415
  1337.7 107.0 %copy-start.66 = (f32[128]{0:T(128)S(1)}, f32[128]{0:T(128)}, u32[]{:S(2)}) copy-start(f32[128]{0:T(128)} %copy-done.65) | copy-start | bytes 1540
  (68 other events, 1643.8 us)
Sparse Core Ops, SparseCore 0:
  71.7 85.0 reduce-scatter.9
  161.5 36.0 all-gather.5
  301.9 22.7 all-gather.7
  329.4 120.3 reduce-scatter.11
  452.0 109.5 reduce-scatter.17
  563.7 110.6 reduce-scatter.13
  683.0 62.6 all-gather.11
  747.2 62.6 all-gather.9
  812.1 85.2 reduce-scatter.19
  899.6 85.7 reduce-scatter.15
  1038.4 33.8 reduce-scatter.21
  1225.1 34.7 reduce-scatter.23
  1263.6 49.3 all-gather.13
  1319.7 85.2 reduce-scatter.25
  1446.0 91.4 all-reduce.12
